TPU v7x, 32 devices: a whole 2x2x4 slice. The times are simulated.
32 devices in a mesh: tm: 2 (over x), lat: 4 (over y, core), lon: 4 (over z).
Axes of the slice: x: 2, y: 2, z: 4, core: 2. Of those that a mesh axis runs over, the one named last changes fastest.
Arguments:
- control: float32 [16, 8, 64, 512], P(None, None, 'lat', 'lon'), may hold values from -6 to 6
- ens_pert: bfloat16 [2, 16, 8, 64, 512], P('tm', None, None, 'lat', 'lon'), may hold values from -6 to 6
- lat_filter: bfloat16 [64, 64], replicated, may hold values from 0 to 2.5, as said below
- lon_filter: bfloat16 [512, 512], replicated, may hold values from 0 to 2.5, as said below
- interp_lat: float32 [128, 18], P('lat'), may hold values from -1.5 to 1.5
- interp_lon: float32 [1024, 130], P('lon'), may hold values from -0.5 to 0.5
- obs_cell: int32 [2, 2, 4, 4, 64], P('tm', None, 'lat', 'lon'), may hold values from 0 to 65535
- obs_count: int32 [2, 2, 4, 4], P('tm', None, 'lat', 'lon'), may hold values from 1 to 64, as said below
- obs_value: float32 [2, 2, 4, 4, 64], P('tm', None, 'lat', 'lon'), may hold values from -18 to 18
- obs_weight: float32 [2, 2, 4, 4, 64], P('tm', None, 'lat', 'lon'), may hold values from 0.1 to 0.4
Outputs:
- gradient: float32 [16, 8, 64, 512], P(None, None, 'lat', 'lon')
Inputs may be any that keep to these rules, and one draw needn't show every extreme that they name: `lat_filter`: within the latitude spreading matrix all entries are non-negative. `lon_filter`: entries are non-negative. `obs_count`: each count is at least 1 and at most 64; in every draw some count equals 64.
All inputs are finite; a program needn't handle non-finite values.
Results may differ from a plain program's by a relative error of at most 0.0003.
Values sent between devices are 32-bit elements; how exact they have to be, the bound alone decides.
No kernel may reach another device: no remote copies, remote signals or barrier semaphores. Data moves between devices by JAX's collectives and lax.ppermute only.
A program may use at most 64 MiB of HBM per device.

v0:
```python
import jax
import jax.numpy as jnp
from jax import lax
from jax.sharding import PartitionSpec as P

HIGHEST = lax.Precision.HIGHEST
DIRECTIONS = ((-1, -1), (-1, 0), (-1, 1), (0, -1), (0, 1), (1, -1), (1, 0), (1, 1))


def extended(array, sides, width):
    for axis, dim in sides:
        size, length = (lax.axis_size(axis), array.shape[dim])
        up = [(i, (i + 1) % size) for i in range(size)]
        down = [(j, i) for i, j in up]
        last = lax.slice_in_dim(array, length - width, length, axis=dim)
        first = lax.slice_in_dim(array, 0, width, axis=dim)
        before = lax.ppermute(last, axis, up)
        after = lax.ppermute(first, axis, down)
        array = jnp.concatenate([before, array, after], axis=dim)
    return array


def spread_field(source, lat_matrix, lon_matrix):
    members, levels, lat_rows, lon_cols = source.shape
    fields = members * levels
    stacked = source.reshape(fields, lat_rows, lon_cols)
    across = jnp.einsum(
        "ab,mbk->mak",
        lat_matrix,
        lax.all_to_all(stacked, "lat", split_axis=0, concat_axis=1, tiled=True),
        precision=HIGHEST,
    )
    halfway = lax.all_to_all(across, "lat", split_axis=1, concat_axis=0, tiled=True)
    column = lax.axis_index("lon") * lon_cols
    portion = lax.all_gather(halfway, "lon", axis=2, tiled=True)
    section = lax.dynamic_slice(lon_matrix, (column, 0), (lon_cols, portion.shape[2]))
    result = jnp.einsum("mak,ck->mac", portion, section, precision=HIGHEST)
    return result.reshape(members, levels, lat_rows, lon_cols)


def rim_region(offset, length):
    if offset < 0:
        return slice(0, 1)
    if offset > 0:
        return slice(length + 1, length + 2)
    return slice(1, length + 1)


def own_cells(offset, length):
    if offset < 0:
        return slice(0, 1)
    if offset > 0:
        return slice(length - 1, length)
    return slice(0, length)


def per_device(
    control,
    ens_pert,
    lat_filter,
    lon_filter,
    interp_lat,
    interp_lon,
    obs_cell,
    obs_count,
    obs_value,
    obs_weight,
):
    lat_matrix = lat_filter.astype(jnp.float32)
    lon_matrix = lon_filter.astype(jnp.float32)
    members = control.shape[0]
    slot_pert = ens_pert[0]
    share = members // lax.axis_size("tm")
    first = lax.axis_index("tm") * share
    mine = lax.dynamic_slice_in_dim(control, first, share, 0)
    spread_mine = spread_field(mine, lat_matrix, lon_matrix)
    weights_here = slot_pert.astype(jnp.float32)
    increment = jnp.sum(
        lax.all_gather(spread_mine, "tm", axis=0, tiled=True) * weights_here, axis=0
    )
    levels, lat_rows, lon_cols = increment.shape
    padded = extended(increment, (("lat", 1), ("lon", 2)), 1)
    lat_band = lax.axis_index("lat")
    edge_rows = jnp.arange(lat_rows + 2)
    dropped = (edge_rows == 0) & (lat_band == 0) | (edge_rows == lat_rows + 1) & (
        lat_band == lax.axis_size("lat") - 1
    )
    keeping = jnp.logical_not(dropped).astype(jnp.float32)[None, :, None]
    padded = padded * keeping
    rowwise = jnp.einsum("ip,lpq->liq", interp_lat, padded, precision=HIGHEST)
    finer = jnp.einsum("liq,jq->lij", rowwise, interp_lon, precision=HIGHEST)
    fine_rows = finer.shape[1]
    fine_cols = finer.shape[2]
    flat_field = finer.reshape(-1)
    slots_range = jnp.arange(obs_cell.shape[-1])
    usable = (slots_range < obs_count[..., None]).astype(jnp.float32)
    package = jnp.stack([obs_cell.astype(jnp.float32), obs_value, obs_weight * usable], axis=0)
    arrived = lax.all_to_all(package, "tm", split_axis=2, concat_axis=1, tiled=True)
    places = arrived[0].reshape(-1).astype(jnp.int32)
    targets = arrived[1].reshape(-1)
    weights = arrived[2].reshape(-1)
    seen = flat_field[places]
    departure = weights * (seen - targets)
    fine_grad = jnp.zeros_like(flat_field).at[places].add(departure)
    fine_grad = fine_grad.reshape(levels, fine_rows, fine_cols)
    pulled = jnp.einsum("jq,lij->liq", interp_lon, fine_grad, precision=HIGHEST)
    coarse_pad = jnp.einsum("ip,liq->lpq", interp_lat, pulled, precision=HIGHEST) * keeping
    outgoing = []
    for lat_step, lon_step in DIRECTIONS:
        holder = jnp.zeros((levels, lat_rows, lon_cols), jnp.float32)
        holder = holder.at[:, own_cells(lat_step, lat_rows), own_cells(lon_step, lon_cols)].set(
            coarse_pad[:, rim_region(lat_step, lat_rows), rim_region(lon_step, lon_cols)]
        )
        outgoing.append(holder)
    bundle = jnp.stack(outgoing, axis=0)
    incoming = extended(bundle, (("lat", 2), ("lon", 3)), 1)
    coarse_grad = coarse_pad[:, 1:-1, 1:-1]
    for number, (lat_step, lon_step) in enumerate(DIRECTIONS):
        coarse_grad = coarse_grad.at[
            :, own_cells(-lat_step, lat_rows), own_cells(-lon_step, lon_cols)
        ].add(incoming[number][:, rim_region(-lat_step, lat_rows), rim_region(-lon_step, lon_cols)])
    weights_here = slot_pert.astype(jnp.float32)
    share_grad = lax.psum_scatter(
        weights_here * coarse_grad[None], "tm", scatter_dimension=0, tiled=True
    )
    adjoint_mine = spread_field(share_grad, lat_matrix.T, lon_matrix.T)
    return control + lax.all_gather(adjoint_mine, "tm", axis=0, tiled=True)


def solution(mesh):
    placed = (
        P(None, None, "lat", "lon"),
        P("tm", None, None, "lat", "lon"),
        P(),
        P(),
        P("lat", None),
        P("lon", None),
        P("tm", None, "lat", "lon", None),
        P("tm", None, "lat", "lon"),
        P("tm", None, "lat", "lon", None),
        P("tm", None, "lat", "lon", None),
    )
    return jax.shard_map(
        per_device,
        mesh=mesh,
        in_specs=placed,
        out_specs=P(None, None, "lat", "lon"),
        check_vma=False,
    )
```

profile of v0, /device:TPU:0, one launch (start us, length us, event | category | flops | bytes accessed | tf_op | source)
XLA Modules:
  0.0 265.9 jit_solution(17152153929202696150)
XLA Ops:
  7.7 12.9 %all_to_all.81 = f32[64,16,128]{2,1,0:T(8,128)S(1)} all-to-all(f32[64,16,128]{2,1,0:T(8,128)S(1)} %bitcast.107), channel_id=1, replica_groups=mesh['tm'=2,'lat'=4,'lon'=4] {'lat'}, dimensions={0} | all-to-all | bytes 1048576 | tf_op jit(solution)/shard_map/all_to_all | solution.py:30
  21.4 11.2 %all_to_all.82 = f32[16,64,128]{2,0,1:T(8,128)S(1)} all-to-all(f32[16,64,128]{2,0,1:T(8,128)S(1)} %copy.43), channel_id=1, replica_groups=mesh['tm'=2,'lat'=4,'lon'=4] {'lat'}, dimensions={1} | all-to-all | bytes 1048576 | tf_op jit(solution)/shard_map/all_to_all | solution.py:33
  33.7 46.6 %all-gather.5.cloned.1.call-done = f32[64,16,512]{2,1,0:T(8,128)} async-done(((f32[64,16,128]{2,1,0:T(8,128)}), f32[64,16,512]{2,1,0:T(8,128)}) %all-gather.5.cloned.1.call-update) | async-done | bytes 2097168 | tf_op jit(solution)/shard_map/all_gather | solution.py:35
  80.3 3.4 %fusion.16 = f32[64,16,128]{2,1,0:T(8,128)} fusion(f32[64,16,512]{2,1,0:T(8,128)} %all-gather.5.cloned.1.call-done, bf16[512,512]{1,0:T(8,128)(2,1)S(1)} %copy-done, s32[]{:T(128)S(6)} %select_n.20), kind=kOutput, calls=%fused_computation.35 | convolution fusion | flops 805306368 | bytes 2752516 | tf_op jit(solution)/shard_map/mak,ck->mac/dot_general | solution.py:37
  85.7 3.2 %all-to-all-start = ((f32[2,1,192]{2,1,0:T(1,128)}), f32[2,1,192]{2,1,0:T(1,128)S(1)}, u32[]{:S(2)}, u32[]{:S(2)}) async-start(f32[2,1,192]{2,1,0:T(1,128)} %reshape.675), calls=%async_computation | async-start | bytes 4096 | tf_op jit(solution)/shard_map/all_to_all | solution.py:98
  90.4 2.2 all-to-all-done
  93.5 9.9 %all-gather.7.cloned.1.call-done = f32[16,8,16,128]{3,2,1,0:T(8,128)} async-done(((f32[8,8,16,128]{3,2,1,0:T(8,128)}), f32[16,8,16,128]{3,2,1,0:T(8,128)}) %all-gather.7.cloned.1.call-update) | async-done | bytes 1048592 | tf_op jit(solution)/shard_map/all_gather | solution.py:79
  103.4 1.3 fusion.1
  104.9 1.7 collective-permute-start.1
  106.6 1.3 collective-permute-done
  108.0 1.5 collective-permute-start.2
  109.5 2.4 collective-permute-start.3
  112.1 3.1 %collective-permute-done.2 = f32[8,18,1]{2,1,0:T(8,128)S(1)} collective-permute-done((f32[8,18,1]{2,1,0:T(8,128)S(1)}, f32[8,18,1]{2,1,0:T(8,128)S(1)}, u32[]{:S(2)}, u32[]{:S(2)}) %collective-permute-start.2) | collective-permute-done | bytes 608 | tf_op jit(solution)/shard_map/ppermute | solution.py:17
  115.1 1.8 collective-permute-done.3
  118.1 1.1 gather_fusion
  119.2 1.3 scatter_custom_fusion
  122.7 1.4 scatter.30
  124.5 1.6 collective-permute-start.5
  126.1 1.6 collective-permute-done.4
  128.4 1.2 collective-permute-start.6
  130.2 2.6 collective-permute-start.7
  132.9 1.4 collective-permute-done.6
  136.6 1.2 scatter-add.40
  138.0 2.1 add_select_fusion
  140.1 1.4 scatter-add.44
  142.8 20.4 %reduce-scatter.2.cloned.1.call-done = f32[8,8,16,128]{3,2,1,0:T(8,128)} async-done(((f32[16,8,16,128]{3,2,1,0:T(8,128)}), f32[8,8,16,128]{3,2,1,0:T(8,128)}) %reduce-scatter.2.cloned.1.call-update) | async-done | bytes 524304 | tf_op jit(solution)/shard_map/reduce_scatter | solution.py:123
  163.2 12.3 %all_to_all.83 = f32[64,16,128]{2,1,0:T(8,128)S(1)} all-to-all(f32[64,16,128]{2,1,0:T(8,128)} %bitcast.117), channel_id=1, replica_groups=mesh['tm'=2,'lat'=4,'lon'=4] {'lat'}, dimensions={0} | all-to-all | bytes 1048576 | tf_op jit(solution)/shard_map/all_to_all | solution.py:30
  176.2 11.2 %all_to_all.84 = f32[16,64,128]{2,0,1:T(8,128)S(1)} all-to-all(f32[16,64,128]{2,0,1:T(8,128)S(1)} %copy.62), channel_id=1, replica_groups=mesh['tm'=2,'lat'=4,'lon'=4] {'lat'}, dimensions={1} | all-to-all | bytes 1048576 | tf_op jit(solution)/shard_map/all_to_all | solution.py:33
  188.5 45.4 %all-gather.9.cloned.1.call-done = f32[64,16,512]{2,1,0:T(8,128)} async-done(((f32[64,16,128]{2,1,0:T(8,128)}), f32[64,16,512]{2,1,0:T(8,128)}) %all-gather.9.cloned.1.call-update) | async-done | bytes 2097168 | tf_op jit(solution)/shard_map/all_gather | solution.py:35
  233.9 3.4 %fusion.14 = f32[64,16,128]{2,1,0:T(8,128)} fusion(f32[64,16,512]{2,1,0:T(8,128)} %all-gather.9.cloned.1.call-done, bf16[512,512]{1,0:T(8,128)(2,1)S(1)} %copy-done, s32[]{:T(128)S(6)} %select_n.20), kind=kOutput, calls=%fused_computation.33 | convolution fusion | flops 805306368 | bytes 2752516 | tf_op jit(solution)/shard_map/mak,ck->mac/dot_general | solution.py:37
  237.4 19.6 %all-gather.11.cloned.1.call-done = f32[16,8,16,128]{3,2,1,0:T(8,128)} async-done(((f32[8,8,16,128]{3,2,1,0:T(8,128)}), f32[16,8,16,128]{3,2,1,0:T(8,128)}) %all-gather.11.cloned.1.call-update) | async-done | bytes 1048592 | tf_op jit(solution)/shard_map/all_gather | solution.py:127
  257.0 2.3 add.122
  (117 shorter events, 17.9 us)
Async XLA Ops:
  6.5 73.7 %copy-start = (bf16[512,512]{1,0:T(8,128)(2,1)S(1)}, bf16[512,512]{1,0:T(8,128)(2,1)}, u32[]{:S(2)}) copy-start(bf16[512,512]{1,0:T(8,128)(2,1)} %param.45) | copy-start | bytes 1572868
  6.5 73.7 %all-gather.5.cloned.1.call-start = ((), (), s32[]{:S(2)}) async-start(), calls=%async_computation.6 | async-start | bytes 2621440 | tf_op jit(solution)/shard_map/all_gather | solution.py:35
  7.7 12.9 %copy-start.4 = (bf16[64,64]{1,0:T(8,128)(2,1)S(1)}, bf16[64,64]{1,0:T(8,128)(2,1)}, u32[]{:S(2)}) copy-start(bf16[64,64]{1,0:T(8,128)(2,1)} %param.44) | copy-start | bytes 24580
  21.4 12.3 %copy-start.6 = (s32[1,2,1,1,64]{4,3,2,1,0:T(1,128)S(1)}, s32[1,2,1,1,64]{4,3,2,1,0:T(1,128)}, u32[]{:S(2)}) copy-start(s32[1,2,1,1,64]{4,3,2,1,0:T(1,128)} %param.48) | copy-start | bytes 1540
  33.6 69.9 %all-gather.7.cloned.1.call-start = ((), (), s32[]{:S(2)}) async-start(), calls=%async_computation.7 | async-start | bytes 1572864 | tf_op jit(solution)/shard_map/all_gather | solution.py:79
  33.6 50.1 %copy-start.7 = (f32[1,2,1,1,64]{4,3,2,1,0:T(1,128)S(1)}, f32[1,2,1,1,64]{4,3,2,1,0:T(1,128)}, u32[]{:S(2)}) copy-start(f32[1,2,1,1,64]{4,3,2,1,0:T(1,128)} %param.51) | copy-start | bytes 1540
  33.6 50.1 %copy-start.9 = (s32[1,2,1,1]{1,3,2,0:T(1,128)S(1)}, s32[1,2,1,1]{1,3,2,0:T(1,128)}, u32[]{:S(2)}) copy-start(s32[1,2,1,1]{1,3,2,0:T(1,128)} %param.49) | copy-start | bytes 28
  33.7 50.2 %copy-start.8 = (f32[1,2,1,1,64]{4,3,2,1,0:T(1,128)S(1)}, f32[1,2,1,1,64]{4,3,2,1,0:T(1,128)}, u32[]{:S(2)}) copy-start(f32[1,2,1,1,64]{4,3,2,1,0:T(1,128)} %param.50) | copy-start | bytes 1540
  33.7 56.0 %copy-start.10 = (s32[3]{0:T(128)S(1)}, s32[3]{0:T(128)}, u32[]{:S(2)}) copy-start(s32[3]{0:T(128)} %constant.430.clone.1) | copy-start | bytes 40
  33.7 69.7 %copy-start.2 = (bf16[1,16,8,16,128]{4,3,2,1,0:T(8,128)(2,1)S(1)}, bf16[1,16,8,16,128]{4,3,2,1,0:T(8,128)(2,1)}, u32[]{:S(2)}) copy-start(bf16[1,16,8,16,128]{4,3,2,1,0:T(8,128)(2,1)} %param.43) | copy-start | bytes 1572868
  83.7 33.2 %copy-start.5 = (f32[32,18]{0,1:T(8,128)S(1)}, f32[32,18]{0,1:T(8,128)}, u32[]{:S(2)}) copy-start(f32[32,18]{0,1:T(8,128)} %param.46) | copy-start | bytes 6916
  85.7 7.0 %all-to-all-start = ((f32[2,1,192]{2,1,0:T(1,128)}), f32[2,1,192]{2,1,0:T(1,128)S(1)}, u32[]{:S(2)}, u32[]{:S(2)}) async-start(f32[2,1,192]{2,1,0:T(1,128)} %reshape.675), calls=%async_computation | async-start | bytes 4096 | tf_op jit(solution)/shard_map/all_to_all | solution.py:98
  88.9 74.3 %reduce-scatter.2.cloned.1.call-start = ((), (), s32[]{:S(2)}) async-start(), calls=%async_computation.8 | async-start | bytes 1572864 | tf_op jit(solution)/shard_map/reduce_scatter | solution.py:123
  93.5 24.0 %copy-start.3 = (f32[256,130]{0,1:T(8,128)S(1)}, f32[256,130]{0,1:T(8,128)}, u32[]{:S(2)}) copy-start(f32[256,130]{0,1:T(8,128)} %param.47) | copy-start | bytes 399364
  104.8 3.1 %collective-permute-start = (f32[8,1,128]{2,1,0:T(1,128)S(1)}, f32[8,1,128]{2,1,0:T(1,128)S(1)}, u32[]{:S(2)}, u32[]{:S(2)}) collective-permute-start(f32[8,1,128]{2,1,0:T(1,128)S(1)} %get-tuple-element.222), channel_id=1, source_target_pairs={{0,4},{4,8},{8,12},{12,0},{1,5},{5,9},{9,13},{13,1},{2,6},{6,10},{... | collective-permute-start | bytes 12296 | tf_op jit(solution)/shard_map/ppermute | solution.py:17
  104.9 3.1 %collective-permute-start.1 = (f32[8,1,128]{2,1,0:T(1,128)S(1)}, f32[8,1,128]{2,1,0:T(1,128)S(1)}, u32[]{:S(2)}, u32[]{:S(2)}) collective-permute-start(f32[8,1,128]{2,1,0:T(1,128)S(1)} %get-tuple-element.223), channel_id=1, source_target_pairs={{4,0},{8,4},{12,8},{0,12},{5,1},{9,5},{13,9},{1,13},{6,2},{10,6},{... | collective-permute-start | bytes 12296 | tf_op jit(solution)/shard_map/ppermute | solution.py:18
  108.0 7.1 %collective-permute-start.2 = (f32[8,18,1]{2,1,0:T(8,128)S(1)}, f32[8,18,1]{2,1,0:T(8,128)S(1)}, u32[]{:S(2)}, u32[]{:S(2)}) collective-permute-start(f32[8,18,1]{2,1,0:T(8,128)S(1)} %get-tuple-element.220), channel_id=1, source_target_pairs={{0,1},{1,2},{2,3},{3,0},{4,5},{5,6},{6,7},{7,4},{8,9},{9,10},{10,1... | collective-permute-start | bytes 1736 | tf_op jit(solution)/shard_map/ppermute | solution.py:17
  109.5 7.5 %collective-permute-start.3 = (f32[8,18,1]{2,1,0:T(8,128)S(1)}, f32[8,18,1]{2,1,0:T(8,128)S(1)}, u32[]{:S(2)}, u32[]{:S(2)}) collective-permute-start(f32[8,18,1]{2,1,0:T(8,128)S(1)} %get-tuple-element.221), channel_id=1, source_target_pairs={{1,0},{2,1},{3,2},{0,3},{5,4},{6,5},{7,6},{4,7},{9,8},{10,9},{11,1... | collective-permute-start | bytes 1736 | tf_op jit(solution)/shard_map/ppermute | solution.py:18
  124.3 3.3 %collective-permute-start.4 = (f32[8,8,1,128]{3,1,2,0:T(8,128)S(1)}, f32[8,8,1,128]{3,1,2,0:T(8,128)S(1)}, u32[]{:S(2)}, u32[]{:S(2)}) collective-permute-start(f32[8,8,1,128]{3,1,2,0:T(8,128)S(1)} %get-tuple-element.211), channel_id=1, source_target_pairs={{0,4},{4,8},{8,12},{12,0},{1,5},{5,9},{9,13},{13,1},{2,6},{6,10},{... | collective-permute-start | bytes 98312 | tf_op jit(solution)/shard_map/ppermute | solution.py:17
  124.5 3.2 %collective-permute-start.5 = (f32[8,8,1,128]{3,1,2,0:T(8,128)S(1)}, f32[8,8,1,128]{3,1,2,0:T(8,128)S(1)}, u32[]{:S(2)}, u32[]{:S(2)}) collective-permute-start(f32[8,8,1,128]{3,1,2,0:T(8,128)S(1)} %get-tuple-element.212), channel_id=1, source_target_pairs={{4,0},{8,4},{12,8},{0,12},{5,1},{9,5},{13,9},{1,13},{6,2},{10,6},{... | collective-permute-start | bytes 98312 | tf_op jit(solution)/shard_map/ppermute | solution.py:18
  128.4 5.9 %collective-permute-start.6 = (f32[8,8,18,1]{2,1,3,0:T(8,128)S(1)}, f32[8,8,18,1]{2,1,3,0:T(8,128)S(1)}, u32[]{:S(2)}, u32[]{:S(2)}) collective-permute-start(f32[8,8,18,1]{2,1,3,0:T(8,128)S(1)} %copy.55), channel_id=1, source_target_pairs={{0,1},{1,2},{2,3},{3,0},{4,5},{5,6},{6,7},{7,4},{8,9},{9,10},{10,1... | collective-permute-start | bytes 13832 | tf_op jit(solution)/shard_map/ppermute | solution.py:17
  130.2 5.0 %collective-permute-start.7 = (f32[8,8,18,1]{2,1,3,0:T(8,128)S(1)}, f32[8,8,18,1]{2,1,3,0:T(8,128)S(1)}, u32[]{:S(2)}, u32[]{:S(2)}) collective-permute-start(f32[8,8,18,1]{2,1,3,0:T(8,128)S(1)} %copy.56), channel_id=1, source_target_pairs={{1,0},{2,1},{3,2},{0,3},{5,4},{6,5},{7,6},{4,7},{9,8},{10,9},{11,1... | collective-permute-start | bytes 13832 | tf_op jit(solution)/shard_map/ppermute | solution.py:18
  142.8 91.2 %all-gather.9.cloned.1.call-start = ((), (), s32[]{:S(2)}) async-start(), calls=%async_computation.9 | async-start | bytes 2621440 | tf_op jit(solution)/shard_map/all_gather | solution.py:35
  188.4 68.6 %copy-start.1 = (f32[16,8,16,128]{3,2,1,0:T(8,128)S(1)}, f32[16,8,16,128]{3,2,1,0:T(8,128)}, u32[]{:S(2)}) copy-start(f32[16,8,16,128]{3,2,1,0:T(8,128)} %param.42) | copy-start | bytes 3145732
  188.4 68.6 %all-gather.11.cloned.1.call-start = ((), (), s32[]{:S(2)}) async-start(), calls=%async_computation.10 | async-start | bytes 1572864 | tf_op jit(solution)/shard_map/all_gather | solution.py:127
Sparse Core Ops, SparseCore 0:
  33.7 46.5 all-gather.4
  83.9 19.5 all-gather.6
  142.9 20.2 reduce-scatter.1
  188.6 45.3 all-gather.8
  237.5 19.4 all-gather.10
where the time goes:
time: 267 us; the launch traced here: 266 us
  waiting for transfers between devices  154 us (58%)
  blocking collectives  47.6 us (18%)
  local copies, waits for them, and re-layouts  15.1 us (6%)
  starting transfers between devices  14.7 us (6%)
  between operations  13.6 us (5%)
  other arithmetic  11.9 us (4%)
  matrix products  9.28 us (3%)
    all_gather x2, waiting for transfers between devices, spread_field(): portion = lax.all_gather(halfway, 'lon', axis=2, tiled=True)  92 us
    all_to_all x2, blocking collectives, spread_field(): lax.all_to_all(stacked, 'lat', split_axis=0, concat_axis=1, tiled=True)  25.1 us
    all_to_all x2, blocking collectives, spread_field(): lax.all_to_all(across, 'lat', split_axis=1, concat_axis=0, tiled=True)  22.4 us
    reduce_scatter x1, waiting for transfers between devices, per_device(): lax.psum_scatter(weights_here * coarse_grad[None], 'tm', scatter_dimensio...  20.4 us
    all_gather x1, waiting for transfers between devices, per_device(): return control + lax.all_gather(adjoint_mine, 'tm', axis=0, tiled=True)  19.6 us
    all_gather x1, waiting for transfers between devices, per_device(): lax.all_gather(spread_mine, 'tm', axis=0, tiled=True) * weights_here  9.88 us
    ppermute x4, starting transfers between devices, extended(): after = lax.ppermute(first, axis, down)  8.39 us
    ppermute x4, waiting for transfers between devices, extended(): before = lax.ppermute(last, axis, up)  7.34 us
  transfers between devices with their start and end apart: 14, of which 12 were waited for; matrix products, arithmetic and copies ran while one was open for 2% of the time, Pallas kernels for 0%

commit v1 on v0

--- a/solution.py
+++ b/solution.py
@@ -5,6 +5,17 @@
 
 HIGHEST = lax.Precision.HIGHEST
 DIRECTIONS = ((-1, -1), (-1, 0), (-1, 1), (0, -1), (0, 1), (1, -1), (1, 0), (1, 1))
+
+
+def gather_by_hops(x, name, along):
+    size = lax.axis_size(name)
+    route = [(i, (i + 1) % size) for i in range(size)]
+    parts = [x]
+    for stride in range(1, size):
+        parts = [lax.ppermute(parts[0], name, route), *parts]
+    whole = jnp.concatenate(parts, axis=along)
+    offset = (lax.axis_index(name) + 1) * parts[-1].shape[along]
+    return jnp.roll(whole, offset, axis=along)
 
 
 def extended(array, sides, width):
@@ -32,7 +43,7 @@
     )
     halfway = lax.all_to_all(across, "lat", split_axis=1, concat_axis=0, tiled=True)
     column = lax.axis_index("lon") * lon_cols
-    portion = lax.all_gather(halfway, "lon", axis=2, tiled=True)
+    portion = gather_by_hops(halfway, "lon", 2)
     section = lax.dynamic_slice(lon_matrix, (column, 0), (lon_cols, portion.shape[2]))
     result = jnp.einsum("mak,ck->mac", portion, section, precision=HIGHEST)
     return result.reshape(members, levels, lat_rows, lon_cols)

time: 267 us -> 257 us (0.963)
  waiting for transfers between devices: 154 us -> 144 us
  starting transfers between devices: 14.7 us -> 17.8 us
    all_gather x2 -> x0, waiting for transfers between devices: 92 us -> none  [spread_field(): portion = lax.all_gather(halfway, 'lon', axis=2, tiled=True)]
    ppermute x0 -> x6, waiting for transfers between devices: none -> 82.5 us  [gather_by_hops(): parts = [lax.ppermute(parts[0], name, route), *parts]]
    ppermute x0 -> x6, starting transfers between devices: none -> 3.19 us  [gather_by_hops(): parts = [lax.ppermute(parts[0], name, route), *parts]]
  transfers between devices with their start and end apart: 14 -> 18, of which waited for: 12 -> 16; matrix products, arithmetic and copies ran while one was open for 2% -> 2% of each run, Pallas kernels for 0% -> 0%
where the time goes in v1:
time: 257 us
  waiting for transfers between devices  144 us (56%)
  blocking collectives  47.6 us (19%)
  starting transfers between devices  17.8 us (7%)
  local copies, waits for them, and re-layouts  13.6 us (5%)
  between operations  13.6 us (5%)
  other arithmetic  11.9 us (5%)
  matrix products  8.44 us (3%)
    ppermute x6, waiting for transfers between devices, gather_by_hops(): parts = [lax.ppermute(parts[0], name, route), *parts]  82.5 us
    all_to_all x2, blocking collectives, spread_field(): lax.all_to_all(stacked, 'lat', split_axis=0, concat_axis=1, tiled=True)  25.1 us
    all_to_all x2, blocking collectives, spread_field(): lax.all_to_all(across, 'lat', split_axis=1, concat_axis=0, tiled=True)  22.4 us
    reduce_scatter x1, waiting for transfers between devices, per_device(): lax.psum_scatter(weights_here * coarse_grad[None], 'tm', scatter_dimensio...  20.4 us
    all_gather x1, waiting for transfers between devices, per_device(): return control + lax.all_gather(adjoint_mine, 'tm', axis=0, tiled=True)  18.9 us
    all_gather x1, waiting for transfers between devices, per_device(): lax.all_gather(spread_mine, 'tm', axis=0, tiled=True) * weights_here  10 us
    ppermute x4, starting transfers between devices, extended(): after = lax.ppermute(first, axis, down)  8.39 us
    ppermute x4, waiting for transfers between devices, extended(): before = lax.ppermute(last, axis, up)  7.21 us
  transfers between devices with their start and end apart: 18, of which 16 were waited for; matrix products, arithmetic and copies ran while one was open for 2% of the time, Pallas kernels for 0%

profile of v1, /device:TPU:0, one launch (start us, length us, event | category | flops | bytes accessed | tf_op | source)
XLA Modules:
  0.0 256.5 jit_solution(712661554091124170)
XLA Ops:
  7.7 12.9 %all_to_all.81 = f32[64,16,128]{2,1,0:T(8,128)S(1)} all-to-all(f32[64,16,128]{2,1,0:T(8,128)S(1)} %bitcast.103), channel_id=1, replica_groups=mesh['tm'=2,'lat'=4,'lon'=4] {'lat'}, dimensions={0} | all-to-all | bytes 1048576 | tf_op jit(solution)/shard_map/all_to_all | solution.py:41
  21.4 11.2 %all_to_all.82 = f32[16,64,128]{2,0,1:T(8,128)S(1)} all-to-all(f32[16,64,128]{2,0,1:T(8,128)S(1)} %copy.43), channel_id=1, replica_groups=mesh['tm'=2,'lat'=4,'lon'=4] {'lat'}, dimensions={1} | all-to-all | bytes 1048576 | tf_op jit(solution)/shard_map/all_to_all | solution.py:44
  32.8 1.6 collective-permute-start
  34.4 13.6 %collective-permute-done = f32[64,16,128]{2,1,0:T(8,128)S(1)} collective-permute-done((f32[64,16,128]{2,1,0:T(8,128)S(1)}, f32[64,16,128]{2,1,0:T(8,128)S(1)}, u32[]{:S(2)}, u32[]{:S(2)}) %collective-permute-start) | collective-permute-done | bytes 524320 | tf_op jit(solution)/shard_map/ppermute | solution.py:15
  48.0 14.3 %collective-permute-done.1 = f32[64,16,128]{2,1,0:T(8,128)S(1)} collective-permute-done((f32[64,16,128]{2,1,0:T(8,128)S(1)}, f32[64,16,128]{2,1,0:T(8,128)S(1)}, u32[]{:S(2)}, u32[]{:S(2)}) %collective-permute-start.1) | collective-permute-done | bytes 524320 | tf_op jit(solution)/shard_map/ppermute | solution.py:15
  62.3 13.4 %collective-permute-done.2 = f32[64,16,128]{2,1,0:T(8,128)S(1)} collective-permute-done((f32[64,16,128]{2,1,0:T(8,128)S(1)}, f32[64,16,128]{2,1,0:T(8,128)S(1)}, u32[]{:S(2)}, u32[]{:S(2)}) %collective-permute-start.2) | collective-permute-done | bytes 524320 | tf_op jit(solution)/shard_map/ppermute | solution.py:15
  75.7 3.0 %fusion.14 = f32[64,16,128]{2,1,0:T(8,128)} fusion(s32[]{:T(128)S(6)} %select_n.34, f32[64,16,128]{2,1,0:T(8,128)S(1)} %collective-permute-done.2, f32[64,16,128]{2,1,0:T(8,128)S(1)} %collective-permute-done.1, f32[64,16,128]{2,1,0:T(8,128)S(1)} %collective-permute-done, f32[64,16,128]{2,1,0:T(8,128)S(1)} %bitcast.112, bf16[512,512]{1,0:T(8,128)(2,1)S(1)} %copy-done, ...), kind=kOutput, calls=%fused_computation.30 | convolution fusion | flops 808976384 | bytes 2752520 | tf_op jit(solution)/shard_map/mak,ck->mac/dot_general | solution.py:48
  80.7 3.2 %all-to-all-start = ((f32[2,1,192]{2,1,0:T(1,128)}), f32[2,1,192]{2,1,0:T(1,128)S(1)}, u32[]{:S(2)}, u32[]{:S(2)}) async-start(f32[2,1,192]{2,1,0:T(1,128)} %reshape.675), calls=%async_computation | async-start | bytes 4096 | tf_op jit(solution)/shard_map/all_to_all | solution.py:109
  85.5 2.2 all-to-all-done
  88.5 10.0 %all-gather.3.cloned.1.call-done = f32[16,8,16,128]{3,2,1,0:T(8,128)} async-done(((f32[8,8,16,128]{3,2,1,0:T(8,128)}), f32[16,8,16,128]{3,2,1,0:T(8,128)}) %all-gather.3.cloned.1.call-update) | async-done | bytes 1048592 | tf_op jit(solution)/shard_map/all_gather | solution.py:90
  100.0 1.7 collective-permute-start.4
  103.2 1.5 collective-permute-start.5
  104.7 2.4 collective-permute-start.6
  107.2 2.9 %collective-permute-done.5 = f32[8,18,1]{2,1,0:T(8,128)S(1)} collective-permute-done((f32[8,18,1]{2,1,0:T(8,128)S(1)}, f32[8,18,1]{2,1,0:T(8,128)S(1)}, u32[]{:S(2)}, u32[]{:S(2)}) %collective-permute-start.5) | collective-permute-done | bytes 608 | tf_op jit(solution)/shard_map/ppermute | solution.py:28
  110.1 2.0 collective-permute-done.6
  117.9 1.4 scatter.30
  119.7 1.6 collective-permute-start.8
  121.3 1.6 collective-permute-done.7
  125.3 2.7 %collective-permute-start.10 = (f32[8,8,18,1]{2,1,3,0:T(8,128)S(1)}, f32[8,8,18,1]{2,1,3,0:T(8,128)S(1)}, u32[]{:S(2)}, u32[]{:S(2)}) collective-permute-start(f32[8,8,18,1]{2,1,3,0:T(8,128)S(1)} %copy.56), channel_id=1, source_target_pairs={{1,0},{2,1},{3,2},{0,3},{5,4},{6,5},{7,6},{4,7},{9,8},{10,9},{11,1... | collective-permute-start | bytes 13832 | tf_op jit(solution)/shard_map/ppermute | solution.py:29
  128.1 1.4 collective-permute-done.9
  133.2 2.1 add_select_fusion
  135.2 1.4 scatter-add.44
  138.1 20.4 %reduce-scatter.2.cloned.1.call-done = f32[8,8,16,128]{3,2,1,0:T(8,128)} async-done(((f32[16,8,16,128]{3,2,1,0:T(8,128)}), f32[8,8,16,128]{3,2,1,0:T(8,128)}) %reduce-scatter.2.cloned.1.call-update) | async-done | bytes 524304 | tf_op jit(solution)/shard_map/reduce_scatter | solution.py:134
  158.6 12.3 %all_to_all.83 = f32[64,16,128]{2,1,0:T(8,128)S(1)} all-to-all(f32[64,16,128]{2,1,0:T(8,128)} %bitcast.117), channel_id=1, replica_groups=mesh['tm'=2,'lat'=4,'lon'=4] {'lat'}, dimensions={0} | all-to-all | bytes 1048576 | tf_op jit(solution)/shard_map/all_to_all | solution.py:41
  171.6 11.2 %all_to_all.84 = f32[16,64,128]{2,0,1:T(8,128)S(1)} all-to-all(f32[16,64,128]{2,0,1:T(8,128)S(1)} %copy.62), channel_id=1, replica_groups=mesh['tm'=2,'lat'=4,'lon'=4] {'lat'}, dimensions={1} | all-to-all | bytes 1048576 | tf_op jit(solution)/shard_map/all_to_all | solution.py:44
  183.0 1.6 collective-permute-start.11
  184.5 13.6 %collective-permute-done.11 = f32[64,16,128]{2,1,0:T(8,128)S(1)} collective-permute-done((f32[64,16,128]{2,1,0:T(8,128)S(1)}, f32[64,16,128]{2,1,0:T(8,128)S(1)}, u32[]{:S(2)}, u32[]{:S(2)}) %collective-permute-start.11) | collective-permute-done | bytes 524320 | tf_op jit(solution)/shard_map/ppermute | solution.py:15
  198.1 14.2 %collective-permute-done.12 = f32[64,16,128]{2,1,0:T(8,128)S(1)} collective-permute-done((f32[64,16,128]{2,1,0:T(8,128)S(1)}, f32[64,16,128]{2,1,0:T(8,128)S(1)}, u32[]{:S(2)}, u32[]{:S(2)}) %collective-permute-start.12) | collective-permute-done | bytes 524320 | tf_op jit(solution)/shard_map/ppermute | solution.py:15
  212.4 13.4 %collective-permute-done.13 = f32[64,16,128]{2,1,0:T(8,128)S(1)} collective-permute-done((f32[64,16,128]{2,1,0:T(8,128)S(1)}, f32[64,16,128]{2,1,0:T(8,128)S(1)}, u32[]{:S(2)}, u32[]{:S(2)}) %collective-permute-start.13) | collective-permute-done | bytes 524320 | tf_op jit(solution)/shard_map/ppermute | solution.py:15
  225.8 3.0 %fusion.4 = f32[64,16,128]{2,1,0:T(8,128)} fusion(s32[]{:T(128)S(6)} %select_n.34, f32[64,16,128]{2,1,0:T(8,128)S(1)} %collective-permute-done.13, f32[64,16,128]{2,1,0:T(8,128)S(1)} %collective-permute-done.12, f32[64,16,128]{2,1,0:T(8,128)S(1)} %collective-permute-done.11, f32[64,16,128]{2,1,0:T(8,128)S(1)} %bitcast.115, ...), kind=kOutput, calls=%fused_computation.22 | convolution fusion | flops 808976384 | bytes 2752520 | tf_op jit(solution)/shard_map/mak,ck->mac/dot_general | solution.py:48
  228.8 18.9 %all-gather.5.cloned.1.call-done = f32[16,8,16,128]{3,2,1,0:T(8,128)} async-done(((f32[8,8,16,128]{3,2,1,0:T(8,128)}), f32[16,8,16,128]{3,2,1,0:T(8,128)}) %all-gather.5.cloned.1.call-update) | async-done | bytes 1048592 | tf_op jit(solution)/shard_map/all_gather | solution.py:138
  247.7 2.3 add.135
  (123 shorter events, 23.8 us)
Async XLA Ops:
  6.5 69.2 %copy-start = (bf16[512,512]{1,0:T(8,128)(2,1)S(1)}, bf16[512,512]{1,0:T(8,128)(2,1)}, u32[]{:S(2)}) copy-start(bf16[512,512]{1,0:T(8,128)(2,1)} %param.47) | copy-start | bytes 1572868
  6.5 92.0 %all-gather.3.cloned.1.call-start = ((), (), s32[]{:S(2)}) async-start(), calls=%async_computation.6 | async-start | bytes 1572864 | tf_op jit(solution)/shard_map/all_gather | solution.py:90
  7.7 12.9 %copy-start.4 = (bf16[64,64]{1,0:T(8,128)(2,1)S(1)}, bf16[64,64]{1,0:T(8,128)(2,1)}, u32[]{:S(2)}) copy-start(bf16[64,64]{1,0:T(8,128)(2,1)} %param.46) | copy-start | bytes 24580
  21.4 40.9 %copy-start.6 = (s32[1,2,1,1,64]{4,3,2,1,0:T(1,128)S(1)}, s32[1,2,1,1,64]{4,3,2,1,0:T(1,128)}, u32[]{:S(2)}) copy-start(s32[1,2,1,1,64]{4,3,2,1,0:T(1,128)} %param.50) | copy-start | bytes 1540
  32.8 15.2 %collective-permute-start = (f32[64,16,128]{2,1,0:T(8,128)S(1)}, f32[64,16,128]{2,1,0:T(8,128)S(1)}, u32[]{:S(2)}, u32[]{:S(2)}) collective-permute-start(f32[64,16,128]{2,1,0:T(8,128)S(1)} %bitcast.111), channel_id=1, source_target_pairs={{0,1},{1,2},{2,3},{3,0},{4,5},{5,6},{6,7},{7,4},{8,9},{9,10},{10,1... | collective-permute-start | bytes 1572872 | tf_op jit(solution)/shard_map/ppermute | solution.py:15
  48.0 14.3 %collective-permute-start.1 = (f32[64,16,128]{2,1,0:T(8,128)S(1)}, f32[64,16,128]{2,1,0:T(8,128)S(1)}, u32[]{:S(2)}, u32[]{:S(2)}) collective-permute-start(f32[64,16,128]{2,1,0:T(8,128)S(1)} %collective-permute-done), channel_id=1, source_target_pairs={{0,1},{1,2},{2,3},{3,0},{4,5},{5,6},{6,7},{7,4},{8,9},{9,10},{10,1... | collective-permute-start | bytes 1572872 | tf_op jit(solution)/shard_map/ppermute | solution.py:15
  62.3 13.4 %collective-permute-start.2 = (f32[64,16,128]{2,1,0:T(8,128)S(1)}, f32[64,16,128]{2,1,0:T(8,128)S(1)}, u32[]{:S(2)}, u32[]{:S(2)}) collective-permute-start(f32[64,16,128]{2,1,0:T(8,128)S(1)} %collective-permute-done.1), channel_id=1, source_target_pairs={{0,1},{1,2},{2,3},{3,0},{4,5},{5,6},{6,7},{7,4},{8,9},{9,10},{10,1... | collective-permute-start | bytes 1572872 | tf_op jit(solution)/shard_map/ppermute | solution.py:15
  62.3 16.5 %copy-start.7 = (f32[1,2,1,1,64]{4,3,2,1,0:T(1,128)S(1)}, f32[1,2,1,1,64]{4,3,2,1,0:T(1,128)}, u32[]{:S(2)}) copy-start(f32[1,2,1,1,64]{4,3,2,1,0:T(1,128)} %param.53) | copy-start | bytes 1540
  62.3 16.5 %copy-start.9 = (s32[1,2,1,1]{1,3,2,0:T(1,128)S(1)}, s32[1,2,1,1]{1,3,2,0:T(1,128)}, u32[]{:S(2)}) copy-start(s32[1,2,1,1]{1,3,2,0:T(1,128)} %param.51) | copy-start | bytes 28
  62.3 16.5 %copy-start.8 = (f32[1,2,1,1,64]{4,3,2,1,0:T(1,128)S(1)}, f32[1,2,1,1,64]{4,3,2,1,0:T(1,128)}, u32[]{:S(2)}) copy-start(f32[1,2,1,1,64]{4,3,2,1,0:T(1,128)} %param.52) | copy-start | bytes 1540
  62.3 22.4 %copy-start.10 = (s32[3]{0:T(128)S(1)}, s32[3]{0:T(128)}, u32[]{:S(2)}) copy-start(s32[3]{0:T(128)} %constant.449.clone.1) | copy-start | bytes 40
  62.3 36.2 %copy-start.2 = (bf16[1,16,8,16,128]{4,3,2,1,0:T(8,128)(2,1)S(1)}, bf16[1,16,8,16,128]{4,3,2,1,0:T(8,128)(2,1)}, u32[]{:S(2)}) copy-start(bf16[1,16,8,16,128]{4,3,2,1,0:T(8,128)(2,1)} %param.45) | copy-start | bytes 1572868
  78.7 33.4 %copy-start.5 = (f32[32,18]{0,1:T(8,128)S(1)}, f32[32,18]{0,1:T(8,128)}, u32[]{:S(2)}) copy-start(f32[32,18]{0,1:T(8,128)} %param.48) | copy-start | bytes 6916
  80.7 7.0 %all-to-all-start = ((f32[2,1,192]{2,1,0:T(1,128)}), f32[2,1,192]{2,1,0:T(1,128)S(1)}, u32[]{:S(2)}, u32[]{:S(2)}) async-start(f32[2,1,192]{2,1,0:T(1,128)} %reshape.675), calls=%async_computation | async-start | bytes 4096 | tf_op jit(solution)/shard_map/all_to_all | solution.py:109
  83.9 74.6 %reduce-scatter.2.cloned.1.call-start = ((), (), s32[]{:S(2)}) async-start(), calls=%async_computation.7 | async-start | bytes 1572864 | tf_op jit(solution)/shard_map/reduce_scatter | solution.py:134
  88.5 24.2 %copy-start.3 = (f32[256,130]{0,1:T(8,128)S(1)}, f32[256,130]{0,1:T(8,128)}, u32[]{:S(2)}) copy-start(f32[256,130]{0,1:T(8,128)} %param.49) | copy-start | bytes 399364
  99.9 3.1 %collective-permute-start.3 = (f32[8,1,128]{2,1,0:T(1,128)S(1)}, f32[8,1,128]{2,1,0:T(1,128)S(1)}, u32[]{:S(2)}, u32[]{:S(2)}) collective-permute-start(f32[8,1,128]{2,1,0:T(1,128)S(1)} %get-tuple-element.223), channel_id=1, source_target_pairs={{0,4},{4,8},{8,12},{12,0},{1,5},{5,9},{9,13},{13,1},{2,6},{6,10},{... | collective-permute-start | bytes 12296 | tf_op jit(solution)/shard_map/ppermute | solution.py:28
  100.0 3.1 %collective-permute-start.4 = (f32[8,1,128]{2,1,0:T(1,128)S(1)}, f32[8,1,128]{2,1,0:T(1,128)S(1)}, u32[]{:S(2)}, u32[]{:S(2)}) collective-permute-start(f32[8,1,128]{2,1,0:T(1,128)S(1)} %get-tuple-element.224), channel_id=1, source_target_pairs={{4,0},{8,4},{12,8},{0,12},{5,1},{9,5},{13,9},{1,13},{6,2},{10,6},{... | collective-permute-start | bytes 12296 | tf_op jit(solution)/shard_map/ppermute | solution.py:29
  103.2 7.0 %collective-permute-start.5 = (f32[8,18,1]{2,1,0:T(8,128)S(1)}, f32[8,18,1]{2,1,0:T(8,128)S(1)}, u32[]{:S(2)}, u32[]{:S(2)}) collective-permute-start(f32[8,18,1]{2,1,0:T(8,128)S(1)} %get-tuple-element.221), channel_id=1, source_target_pairs={{0,1},{1,2},{2,3},{3,0},{4,5},{5,6},{6,7},{7,4},{8,9},{9,10},{10,1... | collective-permute-start | bytes 1736 | tf_op jit(solution)/shard_map/ppermute | solution.py:28
  104.7 7.5 %collective-permute-start.6 = (f32[8,18,1]{2,1,0:T(8,128)S(1)}, f32[8,18,1]{2,1,0:T(8,128)S(1)}, u32[]{:S(2)}, u32[]{:S(2)}) collective-permute-start(f32[8,18,1]{2,1,0:T(8,128)S(1)} %get-tuple-element.222), channel_id=1, source_target_pairs={{1,0},{2,1},{3,2},{0,3},{5,4},{6,5},{7,6},{4,7},{9,8},{10,9},{11,1... | collective-permute-start | bytes 1736 | tf_op jit(solution)/shard_map/ppermute | solution.py:29
  119.5 3.3 %collective-permute-start.7 = (f32[8,8,1,128]{3,1,2,0:T(8,128)S(1)}, f32[8,8,1,128]{3,1,2,0:T(8,128)S(1)}, u32[]{:S(2)}, u32[]{:S(2)}) collective-permute-start(f32[8,8,1,128]{3,1,2,0:T(8,128)S(1)} %get-tuple-element.212), channel_id=1, source_target_pairs={{0,4},{4,8},{8,12},{12,0},{1,5},{5,9},{9,13},{13,1},{2,6},{6,10},{... | collective-permute-start | bytes 98312 | tf_op jit(solution)/shard_map/ppermute | solution.py:28
  119.7 3.2 %collective-permute-start.8 = (f32[8,8,1,128]{3,1,2,0:T(8,128)S(1)}, f32[8,8,1,128]{3,1,2,0:T(8,128)S(1)}, u32[]{:S(2)}, u32[]{:S(2)}) collective-permute-start(f32[8,8,1,128]{3,1,2,0:T(8,128)S(1)} %get-tuple-element.213), channel_id=1, source_target_pairs={{4,0},{8,4},{12,8},{0,12},{5,1},{9,5},{13,9},{1,13},{6,2},{10,6},{... | collective-permute-start | bytes 98312 | tf_op jit(solution)/shard_map/ppermute | solution.py:29
  123.6 5.9 %collective-permute-start.9 = (f32[8,8,18,1]{2,1,3,0:T(8,128)S(1)}, f32[8,8,18,1]{2,1,3,0:T(8,128)S(1)}, u32[]{:S(2)}, u32[]{:S(2)}) collective-permute-start(f32[8,8,18,1]{2,1,3,0:T(8,128)S(1)} %copy.55), channel_id=1, source_target_pairs={{0,1},{1,2},{2,3},{3,0},{4,5},{5,6},{6,7},{7,4},{8,9},{9,10},{10,1... | collective-permute-start | bytes 13832 | tf_op jit(solution)/shard_map/ppermute | solution.py:28
  125.3 5.0 %collective-permute-start.10 = (f32[8,8,18,1]{2,1,3,0:T(8,128)S(1)}, f32[8,8,18,1]{2,1,3,0:T(8,128)S(1)}, u32[]{:S(2)}, u32[]{:S(2)}) collective-permute-start(f32[8,8,18,1]{2,1,3,0:T(8,128)S(1)} %copy.56), channel_id=1, source_target_pairs={{1,0},{2,1},{3,2},{0,3},{5,4},{6,5},{7,6},{4,7},{9,8},{10,9},{11,1... | collective-permute-start | bytes 13832 | tf_op jit(solution)/shard_map/ppermute | solution.py:29
  138.1 109.6 %all-gather.5.cloned.1.call-start = ((), (), s32[]{:S(2)}) async-start(), calls=%async_computation.8 | async-start | bytes 1572864 | tf_op jit(solution)/shard_map/all_gather | solution.py:138
  183.0 15.1 %collective-permute-start.11 = (f32[64,16,128]{2,1,0:T(8,128)S(1)}, f32[64,16,128]{2,1,0:T(8,128)S(1)}, u32[]{:S(2)}, u32[]{:S(2)}) collective-permute-start(f32[64,16,128]{2,1,0:T(8,128)S(1)} %bitcast.114), channel_id=1, source_target_pairs={{0,1},{1,2},{2,3},{3,0},{4,5},{5,6},{6,7},{7,4},{8,9},{9,10},{10,1... | collective-permute-start | bytes 1572872 | tf_op jit(solution)/shard_map/ppermute | solution.py:15
  198.1 14.2 %collective-permute-start.12 = (f32[64,16,128]{2,1,0:T(8,128)S(1)}, f32[64,16,128]{2,1,0:T(8,128)S(1)}, u32[]{:S(2)}, u32[]{:S(2)}) collective-permute-start(f32[64,16,128]{2,1,0:T(8,128)S(1)} %collective-permute-done.11), channel_id=1, source_target_pairs={{0,1},{1,2},{2,3},{3,0},{4,5},{5,6},{6,7},{7,4},{8,9},{9,10},{10,1... | collective-permute-start | bytes 1572872 | tf_op jit(solution)/shard_map/ppermute | solution.py:15
  212.4 13.4 %collective-permute-start.13 = (f32[64,16,128]{2,1,0:T(8,128)S(1)}, f32[64,16,128]{2,1,0:T(8,128)S(1)}, u32[]{:S(2)}, u32[]{:S(2)}) collective-permute-start(f32[64,16,128]{2,1,0:T(8,128)S(1)} %collective-permute-done.12), channel_id=1, source_target_pairs={{0,1},{1,2},{2,3},{3,0},{4,5},{5,6},{6,7},{7,4},{8,9},{9,10},{10,1... | collective-permute-start | bytes 1572872 | tf_op jit(solution)/shard_map/ppermute | solution.py:15
  225.8 21.9 %copy-start.1 = (f32[16,8,16,128]{3,2,1,0:T(8,128)S(1)}, f32[16,8,16,128]{3,2,1,0:T(8,128)}, u32[]{:S(2)}) copy-start(f32[16,8,16,128]{3,2,1,0:T(8,128)} %param.44) | copy-start | bytes 3145732
Sparse Core Ops, SparseCore 0:
  78.9 19.6 all-gather.2
  138.2 20.3 reduce-scatter.1
  228.9 18.7 all-gather.4
